TPU v7x, 128 devices: a whole 4x4x4 slice. The times are simulated.
128 devices in a mesh: tm: 8 (over y_lo, x), space: 16 (over y_hi, z, core).
Axes of the slice: x: 4, y: 4 (y_hi: 2, y_lo: 2; y = y_hi * 2 + y_lo), z: 4, core: 2. Of those that a mesh axis runs over, the one named last changes fastest.
Arguments:
- frames_in: bfloat16 [32, 64, 64, 512], P('tm', 'space'), may hold values from -6 to 6
- spatial_kernel: bfloat16 [3, 3, 512, 512], replicated, may hold values from -0.09375 to 0.09375
- temporal_kernel: bfloat16 [3, 512, 512], replicated, may hold values from -0.15625 to 0.15625
- norm_gain: float32 [512], replicated, may hold values from 0.1 to 1.9
- query_weight: bfloat16 [512, 512], replicated, may hold values from -2 to 2
- key_weight: bfloat16 [512, 512], replicated, may hold values from -2 to 2
- value_weight: bfloat16 [512, 512], replicated, may hold values from -0.25 to 0.25
- out_weight: bfloat16 [512, 512], replicated, may hold values from -0.25 to 0.25
- cotangent: bfloat16 [32, 64, 64, 512], P('tm', 'space'), may hold values from -6 to 6
Outputs:
- encoded: bfloat16 [32, 64, 64, 512], P('tm', 'space')
- kernel_grad: float32 [3, 512, 512], P(None, 'tm', 'space')
All inputs are finite; a program needn't handle non-finite values.
Results may differ from a plain program's by a relative error of at most 0.007.
Values may be sent and summed in bfloat16 or wider, within the bound.
A program may use at most 128 MiB of HBM per device.

v0:
```python
import jax
import jax.numpy as jnp
from jax import lax
from jax.sharding import PartitionSpec as P


def extended_2(cells, sides, width):
    for axis, dim in sides:
        count = lax.axis_size(axis)
        ends = count - 1
        head = lax.slice_in_dim(cells, 0, width, axis=dim)
        tail = lax.slice_in_dim(cells, cells.shape[dim] - width, cells.shape[dim], axis=dim)
        cells = jnp.concatenate(
            [
                lax.ppermute(tail, axis, [(i, (i + 1) % count) for i in range(ends)]),
                cells,
                lax.ppermute(head, axis, [((i + 1) % count, i) for i in range(ends)]),
            ],
            axis=dim,
        )
    return cells


def from_behind(value, axis, steps):
    count = lax.axis_size(axis)
    first, last = (max(0, -steps), min(count, count - steps))
    return lax.ppermute(value, axis, [(source, source + steps) for source in range(first, last)])


def project_all(normed, query_weight, key_weight, value_weight, lead, positions, chans):
    query = (
        jnp.dot(normed, query_weight, preferred_element_type=jnp.float32)
        .astype(jnp.bfloat16)
        .reshape(lead, positions, chans)
    )
    key = (
        jnp.dot(normed, key_weight, preferred_element_type=jnp.float32)
        .astype(jnp.bfloat16)
        .reshape(lead, positions, chans)
    )
    value = (
        jnp.dot(normed, value_weight, preferred_element_type=jnp.float32)
        .astype(jnp.bfloat16)
        .reshape(lead, positions, chans)
    )
    return (query, key, value)


def on_device(
    frames_in,
    spatial_kernel,
    temporal_kernel,
    norm_gain,
    query_weight,
    key_weight,
    value_weight,
    out_weight,
    cotangent,
):
    frames, rows, cols, chans = frames_in.shape
    padded = extended_2(frames_in, (("space", 1),), 1)
    padded = jnp.pad(padded, ((0, 0), (0, 0), (1, 1), (0, 0)))
    spatial = jnp.zeros((frames * rows * cols, chans), jnp.float32)
    for di in range(3):
        for dj in range(3):
            piece = padded[:, di : di + rows, dj : dj + cols, :].reshape(-1, chans)
            spatial = spatial + jnp.dot(
                piece, spatial_kernel[di, dj], preferred_element_type=jnp.float32
            )
    act = jax.nn.silu(spatial).astype(jnp.bfloat16).reshape(frames, rows, cols, chans)
    earlier = from_behind(act[frames - 2 :], "tm", 1)
    extended = jnp.concatenate([earlier, act], axis=0)
    temporal = jnp.zeros((frames * rows * cols, chans), jnp.float32)
    flat_grad = cotangent.reshape(-1, chans)
    grads = []
    for tap in range(3):
        shifted = extended[2 - tap : 2 - tap + frames].reshape(-1, chans)
        temporal = temporal + jnp.dot(
            shifted, temporal_kernel[tap], preferred_element_type=jnp.float32
        )
        grads.append(
            jnp.einsum("nc,nd->cd", shifted, flat_grad, preferred_element_type=jnp.float32)
        )
    partial_grad = jnp.stack(grads, axis=0)
    hidden = (frames_in.reshape(-1, chans).astype(jnp.float32) + temporal).astype(jnp.bfloat16)
    wide = hidden.astype(jnp.float32)
    normed = (
        wide / jnp.sqrt(jnp.mean(wide * wide, axis=1, keepdims=True) + 1e-06) * norm_gain
    ).astype(jnp.bfloat16)
    positions = rows * cols
    query, key, value = project_all(
        normed, query_weight, key_weight, value_weight, frames, positions, chans
    )
    first_frame = lax.axis_index("tm") * frames
    query_frames = first_frame + jnp.arange(frames)
    scale = 1.0 / jnp.sqrt(jnp.float32(chans))
    running_max = jnp.full((frames, positions), -1e30, jnp.float32)
    key_piece = lax.all_gather(key, "tm", axis=0, tiled=True)
    value_piece = lax.all_gather(value, "tm", axis=0, tiled=True)
    scores = (
        jnp.einsum("anc,bnc->abn", query, key_piece, preferred_element_type=jnp.float32) * scale
    )
    key_frames = jnp.arange(key_piece.shape[0])
    allowed = (key_frames[None, :] <= query_frames[:, None])[:, :, None]
    masked = jnp.where(allowed, scores, jnp.float32(-1e30))
    new_max = jnp.maximum(running_max, jnp.max(masked, axis=1))
    expon = jnp.where(allowed, jnp.exp(scores - new_max[:, None, :]), jnp.float32(0.0))
    new_sum = jnp.sum(expon, axis=1)
    new_acc = jnp.einsum("abn,bnc->anc", expon, value_piece.astype(jnp.float32))
    attended = (new_acc / new_sum[:, :, None]).astype(jnp.bfloat16)
    encoded = (
        wide + jnp.dot(attended.reshape(-1, chans), out_weight, preferred_element_type=jnp.float32)
    ).astype(jnp.bfloat16)
    section = lax.psum_scatter(partial_grad, "space", scatter_dimension=2, tiled=True)
    kernel_grad = lax.psum_scatter(section, "tm", scatter_dimension=1, tiled=True)
    return (encoded.reshape(frames, rows, cols, chans), kernel_grad)


def solution(mesh):
    in_specs = (
        P("tm", "space", None, None),
        P(),
        P(),
        P(),
        P(),
        P(),
        P(),
        P(),
        P("tm", "space", None, None),
    )
    out_specs = (P("tm", "space", None, None), P(None, "tm", "space"))
    return jax.shard_map(
        on_device, mesh=mesh, in_specs=in_specs, out_specs=out_specs, check_vma=False
    )
```

profile of v0, /device:TPU:1, one launch (start us, length us, event | category | flops | bytes accessed | tf_op | source)
XLA Modules:
  0.0 465.0 jit_solution(18101736379835137255)
XLA Ops:
  7.2 1.1 fusion.74
  8.4 5.1 %collective-permute-start = (bf16[4,1,64,512]{3,2,1,0:T(8,128)(2,1)S(1)}, bf16[4,1,64,512]{3,2,1,0:T(8,128)(2,1)S(1)}, u32[]{:S(2)}, u32[]{:S(2)}) collective-permute-start(bf16[4,1,64,512]{3,2,1,0:T(8,128)(2,1)S(1)} %get-tuple-element.20), channel_id=1, source_target_pairs={{0,1},{1,2},{2,3},{3,4},{4,5},{5,6},{6,7},{7,8},{8,9},{9,10},{10,1... | collective-permute-start | bytes 786440 | tf_op jit(solution)/shard_map/ppermute | solution.py:15
  13.5 1.9 collective-permute-start.1
  15.4 2.1 fusion.41
  17.5 3.7 collective-permute-done.1
  21.2 0.9 fusion.14
  22.1 1.3 fusion.73
  23.5 0.2 slice-done.1
  23.7 0.7 fusion.37
  24.4 0.7 fusion.39
  25.1 0.7 fusion.43
  25.8 0.7 fusion.45
  26.5 0.7 fusion.49
  27.4 0.7 fusion.35
  28.1 0.7 fusion.47
  28.8 1.6 multiply_convert_fusion
  30.5 3.1 collective-permute-start.2
  33.6 0.7 convolution_bitcast_fusion
  34.3 7.2 %collective-permute-done.2 = bf16[2,4,64,512]{3,2,1,0:T(8,128)(2,1)S(1)} collective-permute-done((bf16[2,4,64,512]{3,2,1,0:T(8,128)(2,1)S(1)}, bf16[2,4,64,512]{3,2,1,0:T(8,128)(2,1)S(1)}, u32[]{:S(2)}, u32[]{:S(2)}) %collective-permute-start.2) | collective-permute-done | bytes 524320 | tf_op jit(solution)/shard_map/ppermute | solution.py:27
  41.5 0.7 convolution_bitcast_fusion.2
  42.3 0.7 convolution_bitcast_fusion.1
  43.0 2.0 pad_maximum_fusion
  45.0 5.1 %copy.30 = f32[3,512,512]{1,0,2:T(4,128)} copy(f32[3,512,512]{2,1,0:T(8,128)} %pad_maximum_fusion) | data formatting | bytes 6291456 | tf_op jit(solution)/shard_map/stack | solution.py:84
  50.2 0.2 reduce-scatter.4.cloned.1.call-start
  50.4 0.4 copy-done.10
  50.8 0.6 dynamic-slice
  52.0 1.7 fusion.29
  53.8 1.4 fusion.24
  55.4 0.7 fusion.27
  56.1 1.0 fusion.5
  57.1 148.1 %all-reduce.4.cloned.1.call-done = f32[3,512,512]{1,0,2:T(4,128)} async-done(((f32[3,512,512]{1,0,2:T(4,128)}), f32[3,512,512]{1,0,2:T(4,128)}) %all-reduce.4.cloned.1.call-update) | async-done | bytes 3145744
  205.3 1.0 constant_dynamic-slice_fusion
  206.3 7.6 %copy.34 = f32[3,512,32]{0,2,1:T(8,128)} copy(f32[3,512,32]{1,0,2:T(4,128)S(1)} %constant_dynamic-slice_fusion) | data formatting | bytes 393216
  213.9 8.8 %reshape.117 = f32[512,96]{1,0:T(8,128)} reshape(f32[512,32,3]{2,1,0:T(8,128)} %bitcast.105) | data formatting | bytes 393216
  222.8 1.8 convolution_convert_fusion.1
  224.6 0.3 all-gather.3.cloned.1.call-start
  224.9 1.7 convolution_convert_fusion.2
  226.8 1.7 convolution_convert_fusion
  228.5 27.6 %reduce-scatter.4.cloned.1.call-done = f32[64,96]{1,0:T(8,128)} async-done(((f32[512,96]{1,0:T(8,128)}), f32[64,96]{1,0:T(8,128)}) %reduce-scatter.4.cloned.1.call-update) | async-done | bytes 24592
  256.0 1.8 reshape.118
  257.9 1.2 copy.31
  259.1 94.7 %all-gather.5.cloned.1.call-done = bf16[32,256,512]{2,1,0:T(8,128)(2,1)} async-done(((bf16[4,256,512]{2,1,0:T(8,128)(2,1)}), bf16[32,256,512]{2,1,0:T(8,128)(2,1)}) %all-gather.5.cloned.1.call-update) | async-done | bytes 8388624 | tf_op jit(solution)/shard_map/all_gather | solution.py:98
  353.8 9.0 %select_reduce_fusion = (f32[4,256]{0,1:T(8,128)S(1)}, f32[4,32,256]{1,0,2:T(4,128)S(1)}) fusion(pred[4,32]{1,0:T(4,128)(4,1)S(1)} %iota_compare_fusion.2, bf16[4,256,512]{2,1,0:T(8,128)(2,1)} %bitcast.128, bf16[32,256,512]{2,1,0:T(8,128)(2,1)} %all-gather.5.cloned.1.call-done), kind=kOutput, calls=%fused_computation.66 | convolution fusion | flops 33651712 | bytes 9572480 | tf_op jit(solution)/shard_map/anc,bnc->abn/dot_general | solution.py:101
  362.8 0.7 fusion.63
  363.5 83.2 %all-gather.3.cloned.1.call-done = bf16[32,256,512]{2,1,0:T(8,128)(2,1)} async-done(((bf16[4,256,512]{2,1,0:T(8,128)(2,1)}), bf16[32,256,512]{2,1,0:T(8,128)(2,1)}) %all-gather.3.cloned.1.call-update) | async-done | bytes 8388624 | tf_op jit(solution)/shard_map/all_gather | solution.py:99
  446.7 9.0 %fusion.9 = bf16[4,256,512]{2,0,1:T(4,128)(2,1)S(1)} fusion(bf16[32,256,512]{2,1,0:T(8,128)(2,1)} %all-gather.3.cloned.1.call-done, f32[4,256]{0,1:T(8,128)S(1)} %fusion.63, f32[4,32,256]{1,0,2:T(4,128)S(1)} %get-tuple-element.25, f32[4,256]{0,1:T(8,128)S(1)} %broadcast_maximum_fusion, pred[4,32]{1,0:T(4,128)(4,1)S(1)} %iota_compare_fusion.2), kind=kOutput, calls=%fused_computation.21 | convolution fusion | flops 34668544 | bytes 9576576 | tf_op jit(solution)/shard_map/abn,bnc->anc/dot_general | solution.py:109
  455.9 0.8 copy-done.8
  456.7 1.7 fusion.8
  (38 shorter events, 1.0 us)
Async XLA Ops:
  7.2 26.4 %copy-start = (bf16[4,4,64,512]{3,2,1,0:T(8,128)(2,1)S(1)}, bf16[4,4,64,512]{3,2,1,0:T(8,128)(2,1)}, u32[]{:S(2)}) copy-start(bf16[4,4,64,512]{3,2,1,0:T(8,128)(2,1)} %param.17) | copy-start | bytes 3145732
  7.2 198.1 %all-reduce.4.cloned.1.call-start = ((), (), s32[]{:S(2)}) async-start(), calls=%async_computation.4 | async-start | bytes 8388608
  8.4 12.8 %copy-start.2 = (bf16[4,4,64,512]{3,2,1,0:T(8,128)(2,1)S(1)}, bf16[4,4,64,512]{3,2,1,0:T(8,128)(2,1)}, u32[]{:S(2)}) copy-start(bf16[4,4,64,512]{3,2,1,0:T(8,128)(2,1)} %param.9) | copy-start | bytes 3145732
  8.4 9.1 %collective-permute-start = (bf16[4,1,64,512]{3,2,1,0:T(8,128)(2,1)S(1)}, bf16[4,1,64,512]{3,2,1,0:T(8,128)(2,1)S(1)}, u32[]{:S(2)}, u32[]{:S(2)}) collective-permute-start(bf16[4,1,64,512]{3,2,1,0:T(8,128)(2,1)S(1)} %get-tuple-element.20), channel_id=1, source_target_pairs={{0,1},{1,2},{2,3},{3,4},{4,5},{5,6},{6,7},{7,8},{8,9},{9,10},{10,1... | collective-permute-start | bytes 786440 | tf_op jit(solution)/shard_map/ppermute | solution.py:15
  13.5 7.7 %collective-permute-start.1 = (bf16[4,1,64,512]{3,2,1,0:T(8,128)(2,1)S(1)}, bf16[4,1,64,512]{3,2,1,0:T(8,128)(2,1)S(1)}, u32[]{:S(2)}, u32[]{:S(2)}) collective-permute-start(bf16[4,1,64,512]{3,2,1,0:T(8,128)(2,1)S(1)} %get-tuple-element.21), channel_id=1, source_target_pairs={{1,0},{2,1},{3,2},{4,3},{5,4},{6,5},{7,6},{8,7},{9,8},{10,9},{11,1... | collective-permute-start | bytes 786440 | tf_op jit(solution)/shard_map/ppermute | solution.py:17
  21.2 2.3 slice-start
  22.1 1.6 slice-start.1
  30.5 11.0 %collective-permute-start.2 = (bf16[2,4,64,512]{3,2,1,0:T(8,128)(2,1)S(1)}, bf16[2,4,64,512]{3,2,1,0:T(8,128)(2,1)S(1)}, u32[]{:S(2)}, u32[]{:S(2)}) collective-permute-start(bf16[2,4,64,512]{3,2,1,0:T(8,128)(2,1)S(1)} %bitcast.127), channel_id=1, source_target_pairs={{0,16},{16,32},{32,48},{48,64},{64,80},{80,96},{96,112},{1,17},{17... | collective-permute-start | bytes 1572872 | tf_op jit(solution)/shard_map/ppermute | solution.py:27
  41.5 0.8 copy-start.4
  50.1 0.7 copy-start.10
  50.2 205.9 %reduce-scatter.4.cloned.1.call-start = ((), (), s32[]{:S(2)}) async-start(), calls=%async_computation.3 | async-start | bytes 294912
  53.8 1.6 copy-start.3
  213.9 8.9 %copy-start.5 = (bf16[512,512]{1,0:T(8,128)(2,1)S(1)}, bf16[512,512]{1,0:T(8,128)(2,1)}, u32[]{:S(2)}) copy-start(bf16[512,512]{1,0:T(8,128)(2,1)} %param.14) | copy-start | bytes 1572868
  213.9 8.9 %copy-start.9 = (f32[512]{0:T(512)S(1)}, f32[512]{0:T(512)}, u32[]{:S(2)}) copy-start(f32[512]{0:T(512)} %param.12) | copy-start | bytes 6148
  222.7 131.1 %all-gather.5.cloned.1.call-start = ((), (), s32[]{:S(2)}) async-start(), calls=%async_computation.2 | async-start | bytes 9437184 | tf_op jit(solution)/shard_map/all_gather | solution.py:98
  222.8 2.1 copy-start.6
  224.6 2.2 copy-start.7
  224.6 222.1 %all-gather.3.cloned.1.call-start = ((), (), s32[]{:S(2)}) async-start(), calls=%async_computation.1 | async-start | bytes 9437184 | tf_op jit(solution)/shard_map/all_gather | solution.py:99
  455.7 1.0 copy-start.8
  455.7 2.7 copy-start.1
Sparse Core Ops, SparseCore 0:
  50.3 154.9 all-reduce.3
  222.8 33.1 reduce-scatter.3
  257.8 95.9 all-gather.4
  356.0 90.6 all-gather.2
where the time goes:
time: 466 us; the launch traced here: 465 us
  waiting for transfers between devices  364 us (78%)
  matrix products  39.1 us (8%)
  local copies, waits for them, and re-layouts  30.6 us (7%)
  between operations  14.7 us (3%)
  starting transfers between devices  10.7 us (2%)
  other arithmetic  5.3 us (1%)
    unnamed x6, waiting for transfers between devices  176 us
    all_gather x1, waiting for transfers between devices, on_device(): key_piece = lax.all_gather(key, 'tm', axis=0, tiled=True)  94.7 us
    all_gather x1, waiting for transfers between devices, on_device(): value_piece = lax.all_gather(value, 'tm', axis=0, tiled=True)  83.2 us
    unnamed x32, local copies, waits for them, and re-layouts  22.8 us
  transfers between devices with their start and end apart: 7, of which 6 were waited for; matrix products, arithmetic and copies ran while one was open for 6% of the time, Pallas kernels for 0%

commit v1 on v0

--- a/solution.py
+++ b/solution.py
@@ -95,7 +95,9 @@
     query_frames = first_frame + jnp.arange(frames)
     scale = 1.0 / jnp.sqrt(jnp.float32(chans))
     running_max = jnp.full((frames, positions), -1e30, jnp.float32)
-    key_piece = lax.all_gather(key, "tm", axis=0, tiled=True)
+    key_piece = jnp.concatenate(
+        lax.all_to_all(jnp.stack([key] * lax.axis_size("tm")), "tm", 0, 0), axis=0
+    )
     value_piece = lax.all_gather(value, "tm", axis=0, tiled=True)
     scores = (
         jnp.einsum("anc,bnc->abn", query, key_piece, preferred_element_type=jnp.float32) * scale

time: 466 us -> 480 us (1.030)
  local copies, waits for them, and re-layouts: 30.6 us -> 58 us
  waiting for transfers between devices: 364 us -> 350 us
  starting transfers between devices: 10.7 us -> 15.8 us
    all_gather x1 -> x0, waiting for transfers between devices: 94.7 us -> none  [on_device(): key_piece = lax.all_gather(key, 'tm', axis=0, tiled=True)]
    unnamed x6 -> x5, waiting for transfers between devices: 176 us -> 223 us
    all_to_all x0 -> x1, waiting for transfers between devices: none -> 27.3 us  [on_device(): lax.all_to_all(jnp.stack([key] * lax.axis_size('tm')), 'tm', 0, 0)]
    reshape x0 -> x1, local copies, waits for them, and re-layouts: none -> 12.5 us  [on_device(): jnp.concatenate(lax.all_to_all(jnp.stack([key] * lax.axis_size('tm')), 't...]
    all_to_all x0 -> x1, local copies, waits for them, and re-layouts: none -> 8.58 us  [on_device(): lax.all_to_all(jnp.stack([key] * lax.axis_size('tm')), 'tm', 0, 0)]
    another operation x0 -> x2, local copies, waits for them, and re-layouts: none -> 6.2 us  [on_device(): jnp.stack([key] * lax.axis_size('tm'))]
    all_gather x1, waiting for transfers between devices: 83.2 us -> 88.8 us  [on_device(): value_piece = lax.all_gather(value, 'tm', axis=0, tiled=True)]
    all_to_all x0 -> x1, starting transfers between devices: none -> 5.4 us  [on_device(): lax.all_to_all(jnp.stack([key] * lax.axis_size('tm')), 'tm', 0, 0)]
  transfers between devices with their start and end apart: 7 -> 7, of which waited for: 6 -> 6; matrix products, arithmetic and copies ran while one was open for 6% -> 10% of each run, Pallas kernels for 0% -> 0%
where the time goes in v1:
time: 480 us; the launch traced here: 479 us
  waiting for transfers between devices  350 us (73%)
  local copies, waits for them, and re-layouts  58 us (12%)
  matrix products  35.3 us (7%)
  starting transfers between devices  15.8 us (3%)
  between operations  14.7 us (3%)
  other arithmetic  5.29 us (1%)
    unnamed x5, waiting for transfers between devices  223 us
    all_gather x1, waiting for transfers between devices, on_device(): value_piece = lax.all_gather(value, 'tm', axis=0, tiled=True)  88.8 us
    all_to_all x1, waiting for transfers between devices, on_device(): lax.all_to_all(jnp.stack([key] * lax.axis_size('tm')), 'tm', 0, 0)  27.3 us
    unnamed x32, local copies, waits for them, and re-layouts  22.8 us
    reshape x1, local copies, waits for them, and re-layouts, on_device(): jnp.concatenate(lax.all_to_all(jnp.stack([key] * lax.axis_size('tm')), 't...  12.5 us
  transfers between devices with their start and end apart: 7, of which 6 were waited for; matrix products, arithmetic and copies ran while one was open for 10% of the time, Pallas kernels for 0%

profile of v1, /device:TPU:1, one launch (start us, length us, event | category | flops | bytes accessed | tf_op | source)
XLA Modules:
  0.0 479.4 jit_solution(9625312876288435312)
XLA Ops:
  7.2 1.1 fusion.67
  8.4 5.1 %collective-permute-start = (bf16[4,1,64,512]{3,2,1,0:T(8,128)(2,1)S(1)}, bf16[4,1,64,512]{3,2,1,0:T(8,128)(2,1)S(1)}, u32[]{:S(2)}, u32[]{:S(2)}) collective-permute-start(bf16[4,1,64,512]{3,2,1,0:T(8,128)(2,1)S(1)} %get-tuple-element.20), channel_id=1, source_target_pairs={{0,1},{1,2},{2,3},{3,4},{4,5},{5,6},{6,7},{7,8},{8,9},{9,10},{10,1... | collective-permute-start | bytes 786440 | tf_op jit(solution)/shard_map/ppermute | solution.py:15
  13.5 1.9 collective-permute-start.1
  15.4 2.1 fusion.34
  17.5 3.7 collective-permute-done.1
  21.2 0.9 fusion.12
  22.1 1.3 fusion.66
  23.7 0.7 fusion.30
  24.4 0.7 fusion.32
  25.1 0.7 fusion.36
  25.8 0.7 fusion.38
  26.5 0.7 fusion.42
  27.4 0.7 fusion.28
  28.1 0.7 fusion.40
  28.8 1.6 multiply_convert_fusion
  30.5 3.1 collective-permute-start.2
  33.6 0.7 convolution_bitcast_fusion
  34.4 7.2 %collective-permute-done.2 = bf16[2,4,64,512]{3,2,1,0:T(8,128)(2,1)S(1)} collective-permute-done((bf16[2,4,64,512]{3,2,1,0:T(8,128)(2,1)S(1)}, bf16[2,4,64,512]{3,2,1,0:T(8,128)(2,1)S(1)}, u32[]{:S(2)}, u32[]{:S(2)}) %collective-permute-start.2) | collective-permute-done | bytes 524320 | tf_op jit(solution)/shard_map/ppermute | solution.py:27
  41.5 0.7 convolution_bitcast_fusion.1
  42.3 0.7 convolution_bitcast_fusion.2
  43.1 2.0 pad_maximum_fusion
  45.0 5.1 %copy.32 = f32[3,512,512]{1,0,2:T(4,128)} copy(f32[3,512,512]{2,1,0:T(8,128)} %pad_maximum_fusion) | data formatting | bytes 6291456 | tf_op jit(solution)/shard_map/stack | solution.py:84
  52.0 1.7 fusion.22
  53.8 1.4 fusion.17
  55.4 0.7 fusion.20
  56.1 1.0 fusion.3
  57.2 148.1 %all-reduce.4.cloned.1.call-done = f32[3,512,512]{1,0,2:T(4,128)} async-done(((f32[3,512,512]{1,0,2:T(4,128)}), f32[3,512,512]{1,0,2:T(4,128)}) %all-reduce.4.cloned.1.call-update) | async-done | bytes 3145744
  205.3 1.0 constant_dynamic-slice_fusion
  206.3 7.6 %copy.36 = f32[3,512,32]{0,2,1:T(8,128)} copy(f32[3,512,32]{1,0,2:T(4,128)S(1)} %constant_dynamic-slice_fusion) | data formatting | bytes 393216
  213.9 8.8 %reshape.119 = f32[512,96]{1,0:T(8,128)} reshape(f32[512,32,3]{2,1,0:T(8,128)} %bitcast.108) | data formatting | bytes 393216
  222.8 1.7 convolution_convert_fusion.2
  224.6 0.8 convolution_convert_fusion.1
  225.4 0.8 copy.27
  226.2 5.4 %stack.15 = bf16[8,4,256,512]{3,1,2,0:T(4,128)(2,1)} broadcast(bf16[4,256,512]{2,0,1:T(4,128)(2,1)S(1)} %copy.27), dimensions={1,2,3} | broadcast | bytes 9437184 | tf_op jit(solution)/shard_map/stack | solution.py:99
  231.6 5.4 %all-to-all-start = ((bf16[8,4,256,512]{3,1,2,0:T(4,128)(2,1)}), bf16[8,4,256,512]{3,1,2,0:T(4,128)(2,1)}, u32[]{:S(2)}, u32[]{:S(2)}) async-start(bf16[8,4,256,512]{3,1,2,0:T(4,128)(2,1)} %stack.15), calls=%async_computation | async-start | bytes 16777216 | tf_op jit(solution)/shard_map/all_to_all | solution.py:99
  237.1 1.8 convolution_convert_fusion
  238.9 75.3 %reduce-scatter.4.cloned.1.call-done = f32[64,96]{1,0:T(8,128)} async-done(((f32[512,96]{1,0:T(8,128)}), f32[64,96]{1,0:T(8,128)}) %reduce-scatter.4.cloned.1.call-update) | async-done | bytes 24592
  314.2 1.8 reshape.120
  316.1 1.2 copy.33
  317.3 27.3 %all-to-all-done = bf16[8,4,256,512]{3,1,2,0:T(4,128)(2,1)} async-done(((bf16[8,4,256,512]{3,1,2,0:T(4,128)(2,1)}), bf16[8,4,256,512]{3,1,2,0:T(4,128)(2,1)}, u32[]{:S(2)}, u32[]{:S(2)}) %all-to-all-start) | async-done | bytes 8388640 | tf_op jit(solution)/shard_map/all_to_all | solution.py:99
  344.6 8.6 %copy.28 = bf16[8,4,256,512]{3,1,0,2:T(4,128)(2,1)} copy(bf16[8,4,256,512]{3,1,2,0:T(4,128)(2,1)} %all-to-all-done) | data formatting | bytes 16777216 | tf_op jit(solution)/shard_map/all_to_all | solution.py:99
  353.2 12.5 %reshape.112 = bf16[32,256,512]{2,0,1:T(8,128)(2,1)} reshape(bf16[8,4,256,512]{3,1,0,2:T(4,128)(2,1)} %copy.28) | data formatting | bytes 16777216 | tf_op jit(solution)/shard_map/reshape | solution.py:98
  365.7 6.0 %select_reduce_fusion = (f32[4,256]{0,1:T(8,128)S(1)}, f32[4,32,256]{1,0,2:T(4,128)S(1)}) fusion(pred[4,32]{1,0:T(4,128)(4,1)S(1)} %iota_compare_fusion.2, bf16[32,256,512]{2,0,1:T(8,128)(2,1)} %reshape.112, bf16[4,256,512]{2,1,0:T(8,128)(2,1)} %bitcast.131), kind=kOutput, calls=%fused_computation.64 | convolution fusion | flops 33651712 | bytes 9572480 | tf_op jit(solution)/shard_map/anc,bnc->abn/dot_general | solution.py:103
  371.7 0.7 fusion.56
  372.4 88.8 %all-gather.2.cloned.1.call-done = bf16[32,256,512]{2,1,0:T(8,128)(2,1)} async-done(((bf16[4,256,512]{2,1,0:T(8,128)(2,1)}), bf16[32,256,512]{2,1,0:T(8,128)(2,1)}) %all-gather.2.cloned.1.call-update) | async-done | bytes 8388624 | tf_op jit(solution)/shard_map/all_gather | solution.py:101
  461.2 9.0 %fusion.7 = bf16[4,256,512]{2,0,1:T(4,128)(2,1)S(1)} fusion(bf16[32,256,512]{2,1,0:T(8,128)(2,1)} %all-gather.2.cloned.1.call-done, f32[4,256]{0,1:T(8,128)S(1)} %fusion.56, f32[4,32,256]{1,0,2:T(4,128)S(1)} %get-tuple-element.25, f32[4,256]{0,1:T(8,128)S(1)} %broadcast_maximum_fusion, pred[4,32]{1,0:T(4,128)(4,1)S(1)} %iota_compare_fusion.2), kind=kOutput, calls=%fused_computation.19 | convolution fusion | flops 34668544 | bytes 9576576 | tf_op jit(solution)/shard_map/abn,bnc->anc/dot_general | solution.py:111
  470.4 0.8 copy-done.8
  471.2 1.7 fusion.6
  (41 shorter events, 2.4 us)
Async XLA Ops:
  7.2 26.5 %copy-start = (bf16[4,4,64,512]{3,2,1,0:T(8,128)(2,1)S(1)}, bf16[4,4,64,512]{3,2,1,0:T(8,128)(2,1)}, u32[]{:S(2)}) copy-start(bf16[4,4,64,512]{3,2,1,0:T(8,128)(2,1)} %param.17) | copy-start | bytes 3145732
  7.2 198.1 %all-reduce.4.cloned.1.call-start = ((), (), s32[]{:S(2)}) async-start(), calls=%async_computation.4 | async-start | bytes 8388608
  8.4 12.8 %copy-start.2 = (bf16[4,4,64,512]{3,2,1,0:T(8,128)(2,1)S(1)}, bf16[4,4,64,512]{3,2,1,0:T(8,128)(2,1)}, u32[]{:S(2)}) copy-start(bf16[4,4,64,512]{3,2,1,0:T(8,128)(2,1)} %param.9) | copy-start | bytes 3145732
  8.4 9.1 %collective-permute-start = (bf16[4,1,64,512]{3,2,1,0:T(8,128)(2,1)S(1)}, bf16[4,1,64,512]{3,2,1,0:T(8,128)(2,1)S(1)}, u32[]{:S(2)}, u32[]{:S(2)}) collective-permute-start(bf16[4,1,64,512]{3,2,1,0:T(8,128)(2,1)S(1)} %get-tuple-element.20), channel_id=1, source_target_pairs={{0,1},{1,2},{2,3},{3,4},{4,5},{5,6},{6,7},{7,8},{8,9},{9,10},{10,1... | collective-permute-start | bytes 786440 | tf_op jit(solution)/shard_map/ppermute | solution.py:15
  13.5 7.7 %collective-permute-start.1 = (bf16[4,1,64,512]{3,2,1,0:T(8,128)(2,1)S(1)}, bf16[4,1,64,512]{3,2,1,0:T(8,128)(2,1)S(1)}, u32[]{:S(2)}, u32[]{:S(2)}) collective-permute-start(bf16[4,1,64,512]{3,2,1,0:T(8,128)(2,1)S(1)} %get-tuple-element.21), channel_id=1, source_target_pairs={{1,0},{2,1},{3,2},{4,3},{5,4},{6,5},{7,6},{8,7},{9,8},{10,9},{11,1... | collective-permute-start | bytes 786440 | tf_op jit(solution)/shard_map/ppermute | solution.py:17
  21.2 2.3 slice-start
  22.1 1.6 slice-start.1
  30.5 11.0 %collective-permute-start.2 = (bf16[2,4,64,512]{3,2,1,0:T(8,128)(2,1)S(1)}, bf16[2,4,64,512]{3,2,1,0:T(8,128)(2,1)S(1)}, u32[]{:S(2)}, u32[]{:S(2)}) collective-permute-start(bf16[2,4,64,512]{3,2,1,0:T(8,128)(2,1)S(1)} %bitcast.130), channel_id=1, source_target_pairs={{0,16},{16,32},{32,48},{48,64},{64,80},{80,96},{96,112},{1,17},{17... | collective-permute-start | bytes 1572872 | tf_op jit(solution)/shard_map/ppermute | solution.py:27
  41.5 0.8 copy-start.4
  50.2 0.7 copy-start.10
  50.2 264.0 %reduce-scatter.4.cloned.1.call-start = ((), (), s32[]{:S(2)}) async-start(), calls=%async_computation.3 | async-start | bytes 294912
  53.8 1.6 copy-start.3
  213.9 8.9 %copy-start.5 = (bf16[512,512]{1,0:T(8,128)(2,1)S(1)}, bf16[512,512]{1,0:T(8,128)(2,1)}, u32[]{:S(2)}) copy-start(bf16[512,512]{1,0:T(8,128)(2,1)} %param.15) | copy-start | bytes 1572868
  213.9 8.9 %copy-start.9 = (f32[512]{0:T(512)S(1)}, f32[512]{0:T(512)}, u32[]{:S(2)}) copy-start(f32[512]{0:T(512)} %param.12) | copy-start | bytes 6148
  222.7 238.4 %all-gather.2.cloned.1.call-start = ((), (), s32[]{:S(2)}) async-start(), calls=%async_computation.2 | async-start | bytes 9437184 | tf_op jit(solution)/shard_map/all_gather | solution.py:101
  222.8 1.8 copy-start.6
  231.6 5.5 %copy-start.7 = (bf16[512,512]{1,0:T(8,128)(2,1)S(1)}, bf16[512,512]{1,0:T(8,128)(2,1)}, u32[]{:S(2)}) copy-start(bf16[512,512]{1,0:T(8,128)(2,1)} %param.13) | copy-start | bytes 1572868
  231.6 113.0 %all-to-all-start = ((bf16[8,4,256,512]{3,1,2,0:T(4,128)(2,1)}), bf16[8,4,256,512]{3,1,2,0:T(4,128)(2,1)}, u32[]{:S(2)}, u32[]{:S(2)}) async-start(bf16[8,4,256,512]{3,1,2,0:T(4,128)(2,1)} %stack.15), calls=%async_computation | async-start | bytes 16777216 | tf_op jit(solution)/shard_map/all_to_all | solution.py:99
  470.2 1.0 copy-start.8
  470.2 2.7 copy-start.1
Sparse Core Ops, SparseCore 0:
  50.3 154.9 all-reduce.3
  222.8 91.3 reduce-scatter.3
  316.5 144.5 all-gather.1
